TPU v7x, 128 devices: a whole 4x4x4 slice. The times are simulated.
128 devices in a mesh: samp: 4 (over z_hi, core), pair: 32 (over y, x, z_lo).
Axes of the slice: x: 4, y: 4, z: 4 (z_hi: 2, z_lo: 2; z = z_hi * 2 + z_lo), core: 2. Of those that a mesh axis runs over, the one named last changes fastest.
Arguments:
- matrix: bfloat16 [32768, 16384], P('samp', 'pair'), may hold values from -48 to 48
- tournament: int32 [2, 32], replicated, may hold values from 0 to 1
Outputs:
- result: bfloat16 [32768, 16384], P('samp', 'pair')
All inputs are finite; a program needn't handle non-finite values.
Results may differ from a plain program's by a relative error of at most 0.008.
Values may be sent and summed in bfloat16 or wider, within the bound.
A program may use at most 128 MiB of HBM per device.

v0:
```python
import jax
import jax.numpy as jnp
from jax import lax
from jax.sharding import PartitionSpec as P

ROUNDS = 2
POLAR_STEPS = 5


coupling = 2.0
start_scale = 6.0


def passed_along(value, axis, by):
    length = lax.axis_size(axis)
    return lax.ppermute(value, axis, [(i, (i + by) % length) for i in range(length)])


def partner_2(value, axis, bit):
    return lax.ppermute(value, axis, [(i, i ^ 1 << bit) for i in range(lax.axis_size(axis))])


def polar_rotation(cross_gram):
    block_width = cross_gram.shape[0]
    frobenius = jnp.sqrt(jnp.sum(cross_gram * cross_gram) + 1e-06)
    coupled = coupling * cross_gram / frobenius
    blank_block = jnp.zeros_like(coupled)
    skew_matrix = jnp.concatenate(
        [jnp.concatenate([blank_block, -coupled], 1), jnp.concatenate([coupled.T, blank_block], 1)],
        0,
    )
    iterate = (jnp.eye(2 * block_width, dtype=coupled.dtype) + skew_matrix) / start_scale
    for iteration in range(POLAR_STEPS):
        rounded = iterate.astype(jnp.bfloat16)
        square = lax.dot_general(
            rounded, rounded, (((0,), (0,)), ((), ())), preferred_element_type=jnp.float32
        ).astype(jnp.bfloat16)
        iterate = 1.5 * iterate - 0.5 * jnp.dot(rounded, square, preferred_element_type=jnp.float32)
    return iterate.astype(jnp.bfloat16)


def local_cross(rows, block_width):
    return lax.dot_general(
        rows[:, :block_width],
        rows[:, block_width:],
        (((0,), (0,)), ((), ())),
        preferred_element_type=jnp.float32,
    )


def pair_gram(current, block_width):
    cross_gram = lax.psum(local_cross(current, block_width).astype(jnp.bfloat16), "samp").astype(
        jnp.float32
    )
    return cross_gram


def shards(matrix, tournament):
    cycle_size = lax.axis_size("pair")
    top_bit = cycle_size.bit_length() - 2
    position = lax.axis_index("pair")
    block_width = matrix.shape[1] // 2
    current = matrix
    for tourney in range(ROUNDS):
        selector = tournament[tourney, position]
        rotation = polar_rotation(pair_gram(current, block_width))
        first_cols = rotation[:, :block_width]
        second_cols = rotation[:, block_width:]
        keep_columns = jnp.where(selector == 1, second_cols, first_cols)
        move_columns = jnp.where(selector == 1, first_cols, second_cols)
        moving_block = jnp.dot(current, move_columns, preferred_element_type=jnp.float32).astype(
            jnp.bfloat16
        )
        arrived = passed_along(moving_block, "pair", 1)
        kept_block = jnp.dot(current, keep_columns, preferred_element_type=jnp.float32).astype(
            jnp.bfloat16
        )
        partner = partner_2(kept_block, "pair", top_bit)
        current = jnp.concatenate([partner, arrived], axis=1)
    return current


def solution(mesh):
    placed = (P("samp", "pair"), P())
    return jax.shard_map(
        shards, mesh=mesh, in_specs=placed, out_specs=P("samp", "pair"), check_vma=False
    )
```

profile of v0, /device:TPU:32, one launch (start us, length us, event | category | flops | bytes accessed | tf_op | source)
XLA Modules:
  0.0 517.8 jit_solution(17959712581910347229)
XLA Ops:
  6.5 5.4 %fusion.17 = bf16[256,256]{1,0:T(8,128)(2,1)} fusion(bf16[8192,512]{1,0:T(8,128)(2,1)} %param.2), kind=kOutput, calls=%fused_computation.44 | convolution fusion | flops 1073807360 | bytes 8519680 | tf_op jit(solution)/shard_map/dot_general | solution.py:43
  13.3 40.2 %all-reduce.7.cloned.1.call-done = bf16[256,256]{1,0:T(8,128)(2,1)} async-done(((bf16[256,256]{1,0:T(8,128)(2,1)}), bf16[256,256]{1,0:T(8,128)(2,1)}) %all-reduce.7.cloned.1.call-update) | async-done | bytes 131088 | tf_op jit(solution)/shard_map/psum | solution.py:52
  53.5 1.6 fusion.51
  55.8 0.9 fusion.50
  57.8 0.9 fusion.13
  58.6 0.9 fusion.12
  59.5 0.9 fusion.11
  60.4 0.9 fusion.15
  61.2 5.8 %fusion = bf16[8192,256]{0,1:T(8,128)(2,1)S(1)} fusion(bf16[8192,512]{1,0:T(8,128)(2,1)} %param.2, pred[]{:T(512)} %bitcast, bf16[512,512]{0,1:T(8,128)(2,1)S(1)} %fusion.15), kind=kOutput, calls=%fused_computation.4 | convolution fusion | flops 2149711872 | bytes 13107201 | tf_op jit(solution)/shard_map/dot_general | solution.py:75
  67.0 5.8 %fusion.1 = bf16[8192,256]{0,1:T(8,128)(2,1)S(1)} fusion(bf16[8192,512]{1,0:T(8,128)(2,1)} %param.2, pred[]{:T(512)} %bitcast, bf16[512,512]{0,1:T(8,128)(2,1)S(1)} %fusion.15), kind=kOutput, calls=%fused_computation.5 | convolution fusion | flops 2149711872 | bytes 13107201 | tf_op jit(solution)/shard_map/dot_general | solution.py:71
  72.8 2.4 collective-permute-start.1
  75.1 3.0 collective-permute-start
  78.7 87.0 %collective-permute-done.1 = bf16[8192,256]{0,1:T(8,128)(2,1)S(1)} collective-permute-done((bf16[8192,256]{0,1:T(8,128)(2,1)S(1)}, bf16[8192,256]{0,1:T(8,128)(2,1)S(1)}, u32[]{:S(2)}, u32[]{:S(2)}) %collective-permute-start.1) | collective-permute-done | bytes 4194336 | tf_op jit(solution)/shard_map/ppermute | solution.py:16
  165.7 93.4 %collective-permute-done = bf16[8192,256]{0,1:T(8,128)(2,1)S(1)} collective-permute-done((bf16[8192,256]{0,1:T(8,128)(2,1)S(1)}, bf16[8192,256]{0,1:T(8,128)(2,1)S(1)}, u32[]{:S(2)}, u32[]{:S(2)}) %collective-permute-start) | collective-permute-done | bytes 4194336 | tf_op jit(solution)/shard_map/ppermute | solution.py:20
  259.1 2.0 copy-done.2
  261.1 1.9 convolution_convert_fusion.14
  263.0 4.8 constant_dynamic-update-slice_fusion.1
  267.8 2.3 constant_dynamic-update-slice_fusion
  270.1 29.1 %all-reduce.9.cloned.1.call-done = bf16[256,256]{1,0:T(8,128)(2,1)} async-done(((bf16[256,256]{1,0:T(8,128)(2,1)}), bf16[256,256]{1,0:T(8,128)(2,1)}) %all-reduce.9.cloned.1.call-update) | async-done | bytes 131088 | tf_op jit(solution)/shard_map/psum | solution.py:52
  299.2 1.6 fusion.53
  301.5 0.9 fusion.71
  302.6 0.9 fusion.9
  303.5 0.9 fusion.8
  304.3 0.9 fusion.7
  305.2 0.9 fusion.6
  306.1 0.9 fusion.16
  306.9 5.8 %convolution_convert_fusion = bf16[8192,256]{1,0:T(8,128)(2,1)S(1)} fusion(bf16[8192,512]{0,1:T(8,128)(2,1)} %constant_dynamic-update-slice_fusion, pred[]{:T(512)} %bitcast.4, bf16[512,512]{0,1:T(8,128)(2,1)S(1)} %fusion.16), kind=kOutput, calls=%fused_computation | convolution fusion | flops 2149711872 | bytes 13107201 | tf_op jit(solution)/shard_map/dot_general | solution.py:71
  312.7 5.8 %convolution_convert_fusion.1 = bf16[8192,256]{1,0:T(8,128)(2,1)S(1)} fusion(bf16[8192,512]{0,1:T(8,128)(2,1)} %constant_dynamic-update-slice_fusion, pred[]{:T(512)} %bitcast.4, bf16[512,512]{0,1:T(8,128)(2,1)S(1)} %fusion.16), kind=kOutput, calls=%fused_computation.1 | convolution fusion | flops 2149711872 | bytes 13107201 | tf_op jit(solution)/shard_map/dot_general | solution.py:75
  318.5 3.1 collective-permute-start.2
  321.6 2.3 collective-permute-start.3
  323.9 179.6 %collective-permute-done.2 = bf16[8192,256]{1,0:T(8,128)(2,1)} collective-permute-done((bf16[8192,256]{1,0:T(8,128)(2,1)S(1)}, bf16[8192,256]{1,0:T(8,128)(2,1)}, u32[]{:S(2)}, u32[]{:S(2)}) %collective-permute-start.2) | collective-permute-done | bytes 4194336 | tf_op jit(solution)/shard_map/ppermute | solution.py:20
  503.5 7.5 %pad_maximum_fusion = bf16[8192,512]{1,0:T(8,128)(2,1)} fusion(bf16[8192,256]{1,0:T(8,128)(2,1)} %collective-permute-done.3, bf16[8192,256]{1,0:T(8,128)(2,1)} %collective-permute-done.2), kind=kLoop, calls=%fused_computation.6 | loop fusion | flops 16777216 | bytes 16777216 | tf_op jit(solution)/shard_map/concatenate | solution.py:79
  (17 shorter events, 1.8 us)
Async XLA Ops:
  6.5 5.5 %copy-start.3 = (s32[2,32]{1,0:T(2,128)S(1)}, s32[2,32]{1,0:T(2,128)}, u32[]{:S(2)}) copy-start(s32[2,32]{1,0:T(2,128)} %param.3) | copy-start | bytes 772
  6.5 47.0 %all-reduce.7.cloned.1.call-start = ((), (), s32[]{:S(2)}) async-start(), calls=%async_computation | async-start | bytes 262144 | tf_op jit(solution)/shard_map/psum | solution.py:52
  12.0 287.2 %all-reduce.9.cloned.1.call-start = ((), (), s32[]{:S(2)}) async-start(), calls=%async_computation.1 | async-start | bytes 262144 | tf_op jit(solution)/shard_map/psum | solution.py:52
  72.8 92.9 %collective-permute-start.1 = (bf16[8192,256]{0,1:T(8,128)(2,1)S(1)}, bf16[8192,256]{0,1:T(8,128)(2,1)S(1)}, u32[]{:S(2)}, u32[]{:S(2)}) collective-permute-start(bf16[8192,256]{0,1:T(8,128)(2,1)S(1)} %fusion.1), channel_id=1, source_target_pairs={{0,1},{1,2},{2,3},{3,4},{4,5},{5,6},{6,7},{7,8},{8,9},{9,10},{10,1... | collective-permute-start | bytes 12582920 | tf_op jit(solution)/shard_map/ppermute | solution.py:16
  75.1 184.0 %collective-permute-start = (bf16[8192,256]{0,1:T(8,128)(2,1)S(1)}, bf16[8192,256]{0,1:T(8,128)(2,1)S(1)}, u32[]{:S(2)}, u32[]{:S(2)}) collective-permute-start(bf16[8192,256]{0,1:T(8,128)(2,1)S(1)} %fusion), channel_id=1, source_target_pairs={{0,16},{1,17},{2,18},{3,19},{4,20},{5,21},{6,22},{7,23},{8,24},{9,... | collective-permute-start | bytes 12582920 | tf_op jit(solution)/shard_map/ppermute | solution.py:20
  165.7 93.4 %copy-start = (bf16[8192,256]{0,1:T(8,128)(2,1)}, bf16[8192,256]{0,1:T(8,128)(2,1)S(1)}, u32[]{:S(2)}) copy-start(bf16[8192,256]{0,1:T(8,128)(2,1)S(1)} %collective-permute-done.1) | copy-start | bytes 12582916
  259.1 2.0 copy-start.2
  263.0 4.8 copy-start.1
  318.5 185.0 %collective-permute-start.2 = (bf16[8192,256]{1,0:T(8,128)(2,1)S(1)}, bf16[8192,256]{1,0:T(8,128)(2,1)}, u32[]{:S(2)}, u32[]{:S(2)}) collective-permute-start(bf16[8192,256]{1,0:T(8,128)(2,1)S(1)} %convolution_convert_fusion.1), channel_id=1, source_target_pairs={{0,16},{1,17},{2,18},{3,19},{4,20},{5,21},{6,22},{7,23},{8,24},{9,... | collective-permute-start | bytes 12582920 | tf_op jit(solution)/shard_map/ppermute | solution.py:20
  321.6 181.9 %collective-permute-start.3 = (bf16[8192,256]{1,0:T(8,128)(2,1)S(1)}, bf16[8192,256]{1,0:T(8,128)(2,1)}, u32[]{:S(2)}, u32[]{:S(2)}) collective-permute-start(bf16[8192,256]{1,0:T(8,128)(2,1)S(1)} %convolution_convert_fusion), channel_id=1, source_target_pairs={{0,1},{1,2},{2,3},{3,4},{4,5},{5,6},{6,7},{7,8},{8,9},{9,10},{10,1... | collective-permute-start | bytes 12582920 | tf_op jit(solution)/shard_map/ppermute | solution.py:16
Sparse Core Ops, SparseCore 0:
  12.1 41.3 all-reduce.6
  263.2 36.0 all-reduce.8
where the time goes:
time: 518 us
  waiting for transfers between devices  429 us (83%)
  matrix products  39.1 us (8%)
  between operations  16.1 us (3%)
  other arithmetic  12.6 us (2%)
  starting transfers between devices  10.8 us (2%)
  local copies, waits for them, and re-layouts  9.95 us (2%)
    ppermute x2, waiting for transfers between devices, partner_2(): lax.ppermute(value, axis, [(i, i ^ 1 << bit) for i in range(lax.axis_size...  273 us
    ppermute x2, waiting for transfers between devices, passed_along(): lax.ppermute(value, axis, [(i, (i + by) % length) for i in range(length)])  87 us
    psum x2, waiting for transfers between devices, pair_gram(): lax.psum(local_cross(current, block_width).astype(jnp.bfloat16), 'samp')  69.3 us
    dot_general x2, matrix products, shards(): jnp.dot(current, keep_columns, preferred_element_type=jnp.float32)  11.6 us
    dot_general x2, matrix products, shards(): jnp.dot(current, move_columns, preferred_element_type=jnp.float32)  11.6 us
  transfers between devices with their start and end apart: 6, of which 5 were waited for; matrix products, arithmetic and copies ran while one was open for 1% of the time, Pallas kernels for 0%

commit v1 on v0

v1 whole, which is shorter than its diff:
```python
import functools

import jax
import jax.numpy as jnp
from jax import lax
from jax.experimental import pallas as pl
from jax.experimental.pallas import tpu as pltpu
from jax.sharding import PartitionSpec as P

POLAR_STEPS = 5
MESH = pl.DeviceIdType.MESH
COUPLING = 2.0
START_SCALE = 6.0
CHUNKS = 8
TILES = 2
F32 = jnp.float32
BF16 = jnp.bfloat16


def over_rows(a, b):
    return lax.dot_general(a, b, (((0,), (0,)), ((), ())), preferred_element_type=F32)


def mul(a, b):
    return jnp.dot(a, b, preferred_element_type=F32)


def half_rows(upper, lower):
    rows = jnp.concatenate([upper, lower], 1) / START_SCALE
    for _ in range(POLAR_STEPS):
        rounded = rows.astype(BF16)
        square = lax.dot_general(
            rounded, rounded, (((1,), (1,)), ((), ())), preferred_element_type=F32
        ).astype(BF16)
        rows = 1.5 * rows - 0.5 * mul(square, rounded)
    return rows.astype(BF16)


def rotation_into(gram, chosen, keep_ref, move_ref):
    width = gram.shape[0]
    coupled = COUPLING * gram / jnp.sqrt(jnp.sum(gram * gram) + 1e-06)
    row = lax.broadcasted_iota(jnp.int32, (width, width), 0)
    eye = (row == lax.broadcasted_iota(jnp.int32, (width, width), 1)).astype(F32)
    top = half_rows(eye, -coupled)
    bottom = half_rows(coupled.T, eye)
    last = chosen == 1
    for i, part in enumerate((top, bottom)):
        first_cols, second_cols = part[:, :width].astype(F32), part[:, width:].astype(F32)
        rows = pl.ds(i * width, width)
        keep_ref[rows, :] = jnp.where(last, second_cols, first_cols).astype(BF16)
        move_ref[rows, :] = jnp.where(last, first_cols, second_cols).astype(BF16)


def kernel(
    tour_ref, y_hbm, out_ref,
    y_ref, kept, moving, arrived, moved, keep_cols, move_cols, acc, wide_in, narrow_out, narrow_in,
    load_sem, send_sem, recv_sem, ex_send, ex_recv,
):
    samp, pair = lax.axis_index("samp"), lax.axis_index("pair")
    slots = lax.axis_size("pair")
    half = slots // 2
    ahead = lax.rem(pair + half + 1, slots)
    behind = lax.rem(pair + half - 1, slots)
    core_peer = samp + 1 - 2 * lax.rem(samp, 2)
    far_peer = lax.rem(samp + 2, 4)
    height, width = kept.shape
    chunk = height // CHUNKS
    tile = chunk // TILES

    loads = [
        pltpu.make_async_copy(
            y_hbm.at[pl.ds(i * chunk, chunk)], y_ref.at[pl.ds(i * chunk, chunk)], load_sem.at[i]
        )
        for i in range(CHUNKS)
    ]
    for load in loads:
        load.start()
    barrier = pltpu.get_barrier_semaphore()
    for where in ({"pair": ahead}, {"pair": behind}, {"samp": core_peer}, {"samp": far_peer}):
        pl.semaphore_signal(barrier, inc=1, device_id=where, device_id_type=MESH)

    def add_gram(a_ref, b_ref, a_cols, b_cols, i):
        def body(t, carry):
            rows = pl.ds(pl.multiple_of(i * chunk + t * tile, tile), tile)
            acc[...] += over_rows(a_ref[rows, a_cols], b_ref[rows, b_cols])
            return carry

        lax.fori_loop(0, TILES, body, 0)

    def summed_gram(step):
        near = pltpu.make_async_remote_copy(
            acc, wide_in.at[step], ex_send.at[2 * step], ex_recv.at[2 * step],
            device_id={"samp": core_peer}, device_id_type=MESH,
        )
        near.start()
        near.wait()
        chip = (acc[...] + wide_in[step]).astype(BF16)
        narrow_out[step] = chip
        far = pltpu.make_async_remote_copy(
            narrow_out.at[step], narrow_in.at[step], ex_send.at[2 * step + 1], ex_recv.at[2 * step + 1],
            device_id={"samp": far_peer}, device_id_type=MESH,
        )
        far.start()
        far.wait()
        return chip.astype(F32) + narrow_in[step].astype(F32)

    def hop(source, target, i, step):
        return pltpu.make_async_remote_copy(
            source, target, send_sem.at[step, i], recv_sem.at[step, i],
            device_id={"pair": ahead}, device_id_type=MESH,
        )

    low, high = pl.ds(0, width), pl.ds(width, width)
    acc[...] = jnp.zeros_like(acc)
    for i in range(CHUNKS):
        loads[i].wait()
        add_gram(y_ref, y_ref, low, high, i)
    pl.semaphore_wait(barrier, 4)
    rotation_into(summed_gram(0), tour_ref[0, pair], keep_cols, move_cols)

    def first_move(i):
        rows = pl.ds(pl.multiple_of(i * chunk, chunk), chunk)
        return hop(moving.at[rows], arrived.at[rows], i, 0)

    def second_move(i):
        rows = pl.ds(pl.multiple_of(i * chunk, chunk), chunk)
        return hop(moved.at[rows], out_ref.at[rows, high], i, 1)

    def rotate_first(cols_ref, to_ref, i):
        def body(t, carry):
            rows = pl.ds(pl.multiple_of(i * chunk + t * tile, tile), tile)
            to_ref[rows, :] = mul(y_ref[rows, :], cols_ref[...]).astype(BF16)
            return carry

        lax.fori_loop(0, TILES, body, 0)

    def rotate_second(cols_ref, to_ref, i):
        def body(t, carry):
            rows = pl.ds(pl.multiple_of(i * chunk + t * tile, tile), tile)
            total = mul(kept[rows, :], cols_ref[low, :]) + mul(arrived[rows, :], cols_ref[high, :])
            to_ref[rows, low] = total.astype(BF16)
            return carry

        lax.fori_loop(0, TILES, body, 0)

    @pl.loop(0, CHUNKS)
    def _(i):
        rotate_first(move_cols, moving, i)
        first_move(i).start()

    @pl.loop(0, CHUNKS)
    def _(i):
        rotate_first(keep_cols, kept, i)

    acc[...] = jnp.zeros_like(acc)

    @pl.loop(0, CHUNKS)
    def _(i):
        first_move(i).wait_recv()
        add_gram(kept, arrived, low, low, i)

    rotation_into(summed_gram(1), tour_ref[1, lax.rem(pair + half, slots)], keep_cols, move_cols)

    @pl.loop(0, CHUNKS)
    def _(i):
        rotate_second(move_cols, moved, i)
        second_move(i).start()

    @pl.loop(0, CHUNKS)
    def _(i):
        rotate_second(keep_cols, out_ref, i)

    @pl.loop(0, CHUNKS)
    def _(i):
        first_move(i).wait_send()
        second_move(i).wait()


def shards(matrix, tournament):
    height, columns = matrix.shape
    width = columns // 2
    block = pltpu.VMEM((height, width), BF16)
    return pl.pallas_call(
        kernel,
        out_shape=jax.ShapeDtypeStruct((height, columns), BF16),
        in_specs=[pl.BlockSpec(memory_space=pltpu.SMEM), pl.BlockSpec(memory_space=pl.ANY)],
        out_specs=pl.BlockSpec(memory_space=pltpu.VMEM),
        scratch_shapes=[
            pltpu.VMEM((height, columns), BF16), block, block, block, block,
            pltpu.VMEM((columns, width), BF16), pltpu.VMEM((columns, width), BF16),
            pltpu.VMEM((width, width), F32), pltpu.VMEM((2, width, width), F32),
            pltpu.VMEM((2, width, width), BF16), pltpu.VMEM((2, width, width), BF16),
            pltpu.SemaphoreType.DMA((CHUNKS,)),
            pltpu.SemaphoreType.DMA((2, CHUNKS)), pltpu.SemaphoreType.DMA((2, CHUNKS)),
            pltpu.SemaphoreType.DMA((4,)), pltpu.SemaphoreType.DMA((4,)),
        ],
        compiler_params=pltpu.CompilerParams(
            collective_id=0, has_side_effects=True, vmem_limit_bytes=56 * 1024 * 1024
        ),
    )(tournament, matrix)


def solution(mesh):
    placed = (P("samp", "pair"), P())
    return jax.shard_map(
        shards, mesh=mesh, in_specs=placed, out_specs=P("samp", "pair"), check_vma=False
    )
```

time: 518 us -> 230 us (0.44)
  waiting for transfers between devices: 429 us -> 0 us
  Pallas kernels: 0 us -> 223 us
  matrix products: 39.1 us -> 0 us
  between operations: 16.1 us -> 0.01 us
  other arithmetic: 12.6 us -> 0 us
  starting transfers between devices: 10.8 us -> 0 us
    ppermute x4 -> x0, waiting for transfers between devices: 360 us -> none  [the longest x2 273 us: partner_2(): lax.ppermute(value, axis, [(i, i ^ 1 << bit) for i in range(lax.axis_size...]
    pallas_call x0 -> x1, Pallas kernels: none -> 223 us  [shards(): pl.pallas_call(kernel, out_shape=jax.ShapeDtypeStruct((height, columns),...]
    psum x2 -> x0, waiting for transfers between devices: 69.3 us -> none  [pair_gram(): lax.psum(local_cross(current, block_width).astype(jnp.bfloat16), 'samp')]
    dot_general x16 -> x0, matrix products: 39.1 us -> none  [the longest x2 11.6 us: shards(): jnp.dot(current, keep_columns, preferred_element_type=jnp.float32)]
    ppermute x4 -> x0, starting transfers between devices: 10.7 us -> none  [the longest x2 6.1 us: partner_2(): lax.ppermute(value, axis, [(i, i ^ 1 << bit) for i in range(lax.axis_size...]
    concatenate x1 -> x0, other arithmetic: 7.47 us -> none  [shards(): current = jnp.concatenate([partner, arrived], axis=1)]
  transfers between devices with their start and end apart: 6 -> 0, of which waited for: 5 -> 0; matrix products, arithmetic and copies ran while one was open for 1% -> 0% of each run, Pallas kernels for 0% -> 0%
where the time goes in v1:
time: 230 us
  Pallas kernels  223 us (97%)
  local copies, waits for them, and re-layouts  7.32 us (3%)
    pallas_call x1, Pallas kernels, shards(): pl.pallas_call(kernel, out_shape=jax.ShapeDtypeStruct((height, columns),...  223 us
    unnamed x1, local copies, waits for them, and re-layouts  7.32 us

profile of v1, /device:TPU:32, one launch (start us, length us, event | category | flops | bytes accessed | tf_op | source)
XLA Modules:
  0.0 230.0 jit_solution(16339554517516192920)
XLA Ops:
  0.0 222.7 %shard_map.28 = bf16[8192,512]{1,0:T(8,128)(2,1)} custom-call(s32[2,32]{1,0:T(2,128)} %tour_ref.1, bf16[8192,512]{1,0:T(8,128)(2,1)} %y_hbm.1), custom_call_target="tpu_custom_call" | custom-call | tf_op jit(solution)/shard_map/pallas_call | solution.py:183
  222.7 7.3 %copy.4 = bf16[8192,512]{1,0:T(8,128)(2,1)} copy(bf16[8192,512]{1,0:T(8,128)(2,1)} %shard_map.28) | data formatting | bytes 16777216

commit v2 on v1

--- a/solution.py
+++ b/solution.py
@@ -182,7 +182,7 @@
     block = pltpu.VMEM((height, width), BF16)
     return pl.pallas_call(
         kernel,
-        out_shape=jax.ShapeDtypeStruct((height, columns), BF16),
+        out_shape=pltpu.VMEM((height, columns), BF16),
         in_specs=[pl.BlockSpec(memory_space=pltpu.SMEM), pl.BlockSpec(memory_space=pl.ANY)],
         out_specs=pl.BlockSpec(memory_space=pltpu.VMEM),
         scratch_shapes=[
@@ -195,7 +195,7 @@
             pltpu.SemaphoreType.DMA((4,)), pltpu.SemaphoreType.DMA((4,)),
         ],
         compiler_params=pltpu.CompilerParams(
-            collective_id=0, has_side_effects=True, vmem_limit_bytes=56 * 1024 * 1024
+            collective_id=0, has_side_effects=True, vmem_limit_bytes=40 * 1024 * 1024
         ),
     )(tournament, matrix)
 

time: 230 us -> 224 us (0.974)
  Pallas kernels: 223 us -> 219 us
  local copies, waits for them, and re-layouts: 7.32 us -> 4.08 us
    pallas_call x1, Pallas kernels: 223 us -> 219 us  [shards(): pl.pallas_call(kernel, out_shape=pltpu.VMEM((height, columns), BF16), in_...]
    unnamed x1 -> x3, local copies, waits for them, and re-layouts: 7.32 us -> 4.08 us
where the time goes in v2:
time: 224 us; the launch traced here: 223 us
  Pallas kernels  219 us (98%)
  local copies, waits for them, and re-layouts  4.08 us (2%)
    pallas_call x1, Pallas kernels, shards(): pl.pallas_call(kernel, out_shape=pltpu.VMEM((height, columns), BF16), in_...  219 us

profile of v2, /device:TPU:32, one launch (start us, length us, event | category | flops | bytes accessed | tf_op | source)
XLA Modules:
  0.0 223.4 jit_solution(5256107780990195900)
XLA Ops:
  0.0 0.0 copy-start
  0.0 0.7 copy-done
  0.7 219.3 %shard_map.28 = bf16[8192,512]{1,0:T(8,128)(2,1)S(1)} custom-call(s32[2,32]{1,0:T(2,128)S(1)} %copy-done, bf16[8192,512]{1,0:T(8,128)(2,1)} %y_hbm.1), custom_call_target="tpu_custom_call" | custom-call | tf_op jit(solution)/shard_map/pallas_call | solution.py:183
  220.0 3.4 %copy.4 = bf16[8192,512]{1,0:T(8,128)(2,1)} copy(bf16[8192,512]{1,0:T(8,128)(2,1)S(1)} %shard_map.28) | data formatting | bytes 16777216
Async XLA Ops:
  0.0 0.7 copy-start

commit v3 on v2

v3 whole, which is shorter than its diff:
```python
import jax
import jax.numpy as jnp
from jax import lax
from jax.experimental import pallas as pl
from jax.experimental.pallas import tpu as pltpu
from jax.sharding import PartitionSpec as P

POLAR_STEPS = 5
MESH = pl.DeviceIdType.MESH
COUPLING = 2.0
START_SCALE = 6.0
CHUNK = 128
TILE = 512
EARLY = 256
PIECES = ((0, 128), (128, 128))
F32 = jnp.float32
BF16 = jnp.bfloat16


def over_rows(a, b):
    return lax.dot_general(a, b, (((0,), (0,)), ((), ())), preferred_element_type=F32)


def mul(a, b):
    return jnp.dot(a, b, preferred_element_type=F32)


def rotation_into(gram, chosen, keep_ref, move_ref):
    width = gram.shape[0]
    coupled = COUPLING * gram / jnp.sqrt(jnp.sum(gram * gram) + 1e-06)
    row = lax.broadcasted_iota(jnp.int32, (width, width), 0)
    eye = (row == lax.broadcasted_iota(jnp.int32, (width, width), 1)).astype(F32)
    halves = [jnp.concatenate([eye, -coupled], 1) / START_SCALE, jnp.concatenate([coupled.T, eye], 1) / START_SCALE]
    for _ in range(POLAR_STEPS):
        rounded = [h.astype(BF16) for h in halves]
        squares = [lax.dot_general(r, r, (((1,), (1,)), ((), ())), preferred_element_type=F32) for r in rounded]
        squares = [(-0.5 * q).astype(BF16) for q in squares]
        halves = [1.5 * h + mul(q, r) for h, q, r in zip(halves, squares, rounded)]
    last = chosen == 1
    for i, h in enumerate(halves):
        first_cols, second_cols = h[:, :width], h[:, width:]
        rows = pl.ds(i * width, width)
        keep_ref[rows, :] = jnp.where(last, second_cols, first_cols).astype(BF16)
        move_ref[rows, :] = jnp.where(last, first_cols, second_cols).astype(BF16)


def kernel(
    tour_hbm, y_hbm, out_ref,
    tour_ref, tour_sem,
    y_ref, kept, moving, arrived, moved, early_in, early_kept, side_in,
    keep_cols, move_cols, far_keep, far_move, acc, wide_in, narrow_out, narrow_in, gram_out, gram_in,
    load_sem, send_sem, recv_sem, ex_send, ex_recv, early_send, early_recv, side_send, side_recv,
):
    samp, pair = lax.axis_index("samp"), lax.axis_index("pair")
    slots = lax.axis_size("pair")
    half = slots // 2

    def slot(by):
        return lax.rem(pair + (by + slots), slots)

    ahead = {"pair": slot(half + 1)}
    side = {"pair": slot(2)}
    core_peer = {"samp": samp + 1 - 2 * lax.rem(samp, 2)}
    far_peer = {"samp": lax.rem(samp + 2, 4)}
    height, width = kept.shape
    low, high = pl.ds(0, width), pl.ds(width, width)
    early = pl.ds(0, EARLY)
    n_early, n_chunks = EARLY // CHUNK, height // CHUNK

    def rows_of(i, size=CHUNK):
        return pl.ds(pl.multiple_of(i * size, size), size)

    def remote(source, target, send, recv, where):
        return pltpu.make_async_remote_copy(
            source, target, send, recv, device_id=where, device_id_type=MESH
        )

    n_loads = load_sem.shape[0]
    part = height // n_loads
    loads = [
        pltpu.make_async_copy(y_hbm.at[pl.ds(i * part, part)], y_ref.at[pl.ds(i * part, part)], load_sem.at[i])
        for i in range(n_loads)
    ]
    for load in loads:
        load.start()
    tour_load = pltpu.make_async_copy(tour_hbm, tour_ref, tour_sem)
    tour_load.start()
    barrier = pltpu.get_barrier_semaphore()
    greeted = (ahead, {"pair": slot(-half - 1)}, side, {"pair": slot(-2)}, core_peer, far_peer)
    for where in greeted:
        pl.semaphore_signal(barrier, inc=1, device_id=where, device_id_type=MESH)

    def summed_gram(step):
        near = remote(acc, wide_in.at[step], ex_send.at[4 * step], ex_recv.at[4 * step], core_peer)
        near.start()
        with jax.named_scope("near"):
            near.wait()
        chip = (acc[...] + wide_in[step]).astype(BF16)
        narrow_out[step] = chip
        far = remote(
            narrow_out.at[step], narrow_in.at[step], ex_send.at[4 * step + 1], ex_recv.at[4 * step + 1], far_peer
        )
        far.start()
        with jax.named_scope("far"):
            far.wait()
        total = (chip.astype(F32) + narrow_in[step].astype(F32)).astype(BF16)
        gram_out[step] = total
        passed_gram(step).start()
        if step == 0:
            early_move(1).start()
        return total.astype(F32)

    core = lax.rem(samp, 2)
    my_part = pl.ds(pl.multiple_of(core * (width // 2), width // 2), width // 2)

    def passed_gram(step):
        source, target = gram_out.at[step, my_part], gram_in.at[step, my_part]
        return remote(source, target, ex_send.at[4 * step + 2], ex_recv.at[4 * step + 2], ahead)

    def gram_from_behind(step):
        passed_gram(step).wait()
        half_gram = gram_in.at[step, my_part]
        share = remote(half_gram, half_gram, ex_send.at[4 * step + 3], ex_recv.at[4 * step + 3], core_peer)
        share.start()
        share.wait()
        return gram_in[step].astype(F32)

    def early_move(k):
        rows = pl.ds(*PIECES[k])
        return remote(y_hbm.at[rows], early_in.at[rows], early_send.at[k], early_recv.at[k], ahead)

    side_move = remote(moving.at[early], side_in, side_send, side_recv, side)

    def first_move(i):
        return remote(moving.at[rows_of(i)], arrived.at[rows_of(i)], send_sem.at[0, i], recv_sem.at[0, i], ahead)

    def second_move(i):
        return remote(
            moved.at[rows_of(i)], out_ref.at[rows_of(i), high], send_sem.at[1, i], recv_sem.at[1, i], ahead
        )

    def rotate_first(from_ref, cols_ref, to_ref, rows):
        to_ref[rows, :] = mul(from_ref[rows, :], cols_ref[...]).astype(BF16)

    def rotate_second(kept_ref, moved_ref, cols_ref, to_ref, to_cols, rows):
        total = mul(kept_ref[rows, :], cols_ref[low, :]) + mul(moved_ref[rows, :], cols_ref[high, :])
        to_ref[rows, to_cols] = total.astype(BF16)

    with jax.named_scope("gram0"):
        acc[...] = jnp.zeros_like(acc)
        for i in range(n_loads):
            loads[i].wait()
            rows = pl.ds(i * part, part)
            acc[...] += over_rows(y_ref[rows, low], y_ref[rows, high])
            if i == 0:
                tour_load.wait()
                pl.semaphore_wait(barrier, len(greeted))
                early_move(0).start()

    with jax.named_scope("exch0"):
        gram = summed_gram(0)
    with jax.named_scope("polar0"):
        rotation_into(gram, tour_ref[0, pair], keep_cols, move_cols)
    with jax.named_scope("moves0"):

        @pl.loop(n_early, n_chunks)
        def _(i):
            rotate_first(y_ref, move_cols, moving, rows_of(i))
            first_move(i).start()

        rotate_first(y_ref, move_cols, moving, early)

        @pl.loop(0, height // TILE)
        def _(i):
            rotate_first(y_ref, keep_cols, kept, rows_of(i, TILE))

    with jax.named_scope("gwait0"):
        gram = gram_from_behind(0)
    with jax.named_scope("farpolar0"):
        rotation_into(gram, tour_ref[0, slot(-half - 1)], far_keep, far_move)
    with jax.named_scope("early"):
        for k in range(len(PIECES)):
            early_move(k).wait()
        rotate_first(early_in, far_keep, early_kept, early)
        rotate_first(early_in, far_move, arrived, early)
        acc[...] = over_rows(kept[early, :], arrived[early, :])

    with jax.named_scope("gram1"):

        @pl.loop(n_early, n_chunks)
        def _(i):
            first_move(i).wait_recv()
            acc[...] += over_rows(kept[rows_of(i), :], arrived[rows_of(i), :])

    with jax.named_scope("exch1"):
        side_move.start()
        gram = summed_gram(1)
    with jax.named_scope("polar1"):
        rotation_into(gram, tour_ref[1, slot(half)], keep_cols, move_cols)
    with jax.named_scope("moves1"):

        @pl.loop(n_early, n_chunks)
        def _(i):
            rotate_second(kept, arrived, move_cols, moved, low, rows_of(i))
            second_move(i).start()

        @pl.loop(0, height // TILE)
        def _(i):
            rotate_second(kept, arrived, keep_cols, out_ref, low, rows_of(i, TILE))

    with jax.named_scope("gwait1"):
        gram = gram_from_behind(1)
    with jax.named_scope("farpolar1"):
        rotation_into(gram, tour_ref[1, slot(-1)], far_keep, far_move)
    with jax.named_scope("side"):
        side_move.wait()
        rotate_second(early_kept, side_in, far_move, out_ref, high, early)

    with jax.named_scope("last"):

        @pl.loop(n_early, n_chunks)
        def _(i):
            first_move(i).wait_send()
            second_move(i).wait()


def shards(matrix, tournament):
    height, columns = matrix.shape
    width = columns // 2
    block = pltpu.VMEM((height, width), BF16)
    short = pltpu.VMEM((EARLY, width), BF16)
    cols = pltpu.VMEM((columns, width), BF16)
    grams = pltpu.VMEM((2, width, width), BF16)
    copies = pltpu.SemaphoreType.DMA((2, height // CHUNK))
    one = pltpu.SemaphoreType.DMA
    return pl.pallas_call(
        kernel,
        out_shape=pltpu.VMEM((height, columns), BF16),
        in_specs=[pl.BlockSpec(memory_space=pl.ANY), pl.BlockSpec(memory_space=pl.ANY)],
        out_specs=pl.BlockSpec(memory_space=pltpu.VMEM),
        scratch_shapes=[
            pltpu.SMEM(tournament.shape, jnp.int32), pltpu.SemaphoreType.DMA,
            pltpu.VMEM((height, columns), BF16), block, block, block, block,
            pltpu.VMEM((EARLY, columns), BF16), short, short, cols, cols, cols, cols,
            pltpu.VMEM((width, width), F32), pltpu.VMEM((2, width, width), F32), grams, grams, grams, grams,
            pltpu.SemaphoreType.DMA((4,)), copies, copies,
            pltpu.SemaphoreType.DMA((8,)), pltpu.SemaphoreType.DMA((8,)),
            one((len(PIECES),)), one((len(PIECES),)), one, one,
        ],
        compiler_params=pltpu.CompilerParams(
            collective_id=0, has_side_effects=True, vmem_limit_bytes=40 * 1024 * 1024
        ),
    )(tournament, matrix)


def solution(mesh):
    placed = (P("samp", "pair"), P())
    return jax.shard_map(
        shards, mesh=mesh, in_specs=placed, out_specs=P("samp", "pair"), check_vma=False
    )
```

time: 224 us -> 220 us (0.982)
  Pallas kernels: 219 us -> 215 us
    pallas_call x1, Pallas kernels: 219 us -> 215 us  [shards(): pl.pallas_call(kernel, out_shape=pltpu.VMEM((height, columns), BF16), in_...]
where the time goes in v3:
time: 220 us; the launch traced here: 219 us
  Pallas kernels  215 us (98%)
  local copies, waits for them, and re-layouts  4.08 us (2%)
    pallas_call x1, Pallas kernels, shards(): pl.pallas_call(kernel, out_shape=pltpu.VMEM((height, columns), BF16), in_...  215 us

profile of v3, /device:TPU:32, one launch (start us, length us, event | category | flops | bytes accessed | tf_op | source)
XLA Modules:
  0.0 219.4 jit_solution(1291248430855692502)
XLA Ops:
  0.0 0.0 copy-start
  0.0 0.7 copy-done
  0.7 215.4 %shard_map.28 = bf16[8192,512]{1,0:T(8,128)(2,1)S(1)} custom-call(s32[2,32]{1,0:T(2,128)S(1)} %copy-done, bf16[8192,512]{1,0:T(8,128)(2,1)} %y_hbm.1), custom_call_target="tpu_custom_call" | custom-call | tf_op jit(solution)/shard_map/pallas_call | solution.py:236
  216.0 3.4 %copy.4 = bf16[8192,512]{1,0:T(8,128)(2,1)} copy(bf16[8192,512]{1,0:T(8,128)(2,1)S(1)} %shard_map.28) | data formatting | bytes 16777216
Async XLA Ops:
  0.0 0.7 copy-start

commit v4 on v3

--- a/solution.py
+++ b/solution.py
@@ -25,7 +25,8 @@
     return jnp.dot(a, b, preferred_element_type=F32)
 
 
-def rotation_into(gram, chosen, keep_ref, move_ref):
+def rotation_into(gram_ref, chosen, keep_ref, move_ref):
+    gram = gram_ref[...].astype(F32)
     width = gram.shape[0]
     coupled = COUPLING * gram / jnp.sqrt(jnp.sum(gram * gram) + 1e-06)
     row = lax.broadcasted_iota(jnp.int32, (width, width), 0)
@@ -70,6 +71,13 @@
     def rows_of(i, size=CHUNK):
         return pl.ds(pl.multiple_of(i * size, size), size)
 
+    def stage(name):
+        def run(body):
+            with jax.named_scope(name):
+                pl.when(samp >= 0)(body)
+
+        return run
+
     def remote(source, target, send, recv, where):
         return pltpu.make_async_remote_copy(
             source, target, send, recv, device_id=where, device_id_type=MESH
@@ -93,22 +101,19 @@
     def summed_gram(step):
         near = remote(acc, wide_in.at[step], ex_send.at[4 * step], ex_recv.at[4 * step], core_peer)
         near.start()
-        with jax.named_scope("near"):
-            near.wait()
+        near.wait()
         chip = (acc[...] + wide_in[step]).astype(BF16)
         narrow_out[step] = chip
         far = remote(
             narrow_out.at[step], narrow_in.at[step], ex_send.at[4 * step + 1], ex_recv.at[4 * step + 1], far_peer
         )
         far.start()
-        with jax.named_scope("far"):
-            far.wait()
+        far.wait()
         total = (chip.astype(F32) + narrow_in[step].astype(F32)).astype(BF16)
         gram_out[step] = total
         passed_gram(step).start()
         if step == 0:
             early_move(1).start()
-        return total.astype(F32)
 
     core = lax.rem(samp, 2)
     my_part = pl.ds(pl.multiple_of(core * (width // 2), width // 2), width // 2)
@@ -123,7 +128,6 @@
         share = remote(half_gram, half_gram, ex_send.at[4 * step + 3], ex_recv.at[4 * step + 3], core_peer)
         share.start()
         share.wait()
-        return gram_in[step].astype(F32)
 
     def early_move(k):
         rows = pl.ds(*PIECES[k])
@@ -157,11 +161,14 @@
                 pl.semaphore_wait(barrier, len(greeted))
                 early_move(0).start()
 
-    with jax.named_scope("exch0"):
-        gram = summed_gram(0)
-    with jax.named_scope("polar0"):
-        rotation_into(gram, tour_ref[0, pair], keep_cols, move_cols)
-    with jax.named_scope("moves0"):
+    @stage("exch0")
+    def _():
+        summed_gram(0)
+    @stage("polar0")
+    def _():
+        rotation_into(gram_out.at[0], tour_ref[0, pair], keep_cols, move_cols)
+    @stage("moves0")
+    def _():
 
         @pl.loop(n_early, n_chunks)
         def _(i):
@@ -174,30 +181,37 @@
         def _(i):
             rotate_first(y_ref, keep_cols, kept, rows_of(i, TILE))
 
-    with jax.named_scope("gwait0"):
-        gram = gram_from_behind(0)
-    with jax.named_scope("farpolar0"):
-        rotation_into(gram, tour_ref[0, slot(-half - 1)], far_keep, far_move)
-    with jax.named_scope("early"):
+    @stage("gwait0")
+    def _():
+        gram_from_behind(0)
+    @stage("farpolar0")
+    def _():
+        rotation_into(gram_in.at[0], tour_ref[0, slot(-half - 1)], far_keep, far_move)
+    @stage("early")
+    def _():
         for k in range(len(PIECES)):
             early_move(k).wait()
         rotate_first(early_in, far_keep, early_kept, early)
         rotate_first(early_in, far_move, arrived, early)
         acc[...] = over_rows(kept[early, :], arrived[early, :])
 
-    with jax.named_scope("gram1"):
+    @stage("gram1")
+    def _():
 
         @pl.loop(n_early, n_chunks)
         def _(i):
             first_move(i).wait_recv()
             acc[...] += over_rows(kept[rows_of(i), :], arrived[rows_of(i), :])
 
-    with jax.named_scope("exch1"):
+    @stage("exch1")
+    def _():
         side_move.start()
-        gram = summed_gram(1)
-    with jax.named_scope("polar1"):
-        rotation_into(gram, tour_ref[1, slot(half)], keep_cols, move_cols)
-    with jax.named_scope("moves1"):
+        summed_gram(1)
+    @stage("polar1")
+    def _():
+        rotation_into(gram_out.at[1], tour_ref[1, slot(half)], keep_cols, move_cols)
+    @stage("moves1")
+    def _():
 
         @pl.loop(n_early, n_chunks)
         def _(i):
@@ -208,15 +222,19 @@
         def _(i):
             rotate_second(kept, arrived, keep_cols, out_ref, low, rows_of(i, TILE))
 
-    with jax.named_scope("gwait1"):
-        gram = gram_from_behind(1)
-    with jax.named_scope("farpolar1"):
-        rotation_into(gram, tour_ref[1, slot(-1)], far_keep, far_move)
-    with jax.named_scope("side"):
+    @stage("gwait1")
+    def _():
+        gram_from_behind(1)
+    @stage("farpolar1")
+    def _():
+        rotation_into(gram_in.at[1], tour_ref[1, slot(-1)], far_keep, far_move)
+    @stage("side")
+    def _():
         side_move.wait()
         rotate_second(early_kept, side_in, far_move, out_ref, high, early)
 
-    with jax.named_scope("last"):
+    @stage("last")
+    def _():
 
         @pl.loop(n_early, n_chunks)
         def _(i):

time: 220 us -> 217 us (0.986)
  Pallas kernels: 215 us -> 212 us
    pallas_call x1, Pallas kernels: 215 us -> 212 us  [shards(): pl.pallas_call(kernel, out_shape=pltpu.VMEM((height, columns), BF16), in_...]
where the time goes in v4:
time: 217 us; the launch traced here: 216 us
  Pallas kernels  212 us (98%)
  local copies, waits for them, and re-layouts  4.08 us (2%)
    pallas_call x1, Pallas kernels, shards(): pl.pallas_call(kernel, out_shape=pltpu.VMEM((height, columns), BF16), in_...  212 us

profile of v4, /device:TPU:32, one launch (start us, length us, event | category | flops | bytes accessed | tf_op | source)
XLA Modules:
  0.0 216.2 jit_solution(3730785349871232009)
XLA Ops:
  0.0 0.0 copy-start
  0.0 0.7 copy-done
  0.7 212.1 %shard_map.28 = bf16[8192,512]{1,0:T(8,128)(2,1)S(1)} custom-call(s32[2,32]{1,0:T(2,128)S(1)} %copy-done, bf16[8192,512]{1,0:T(8,128)(2,1)} %y_hbm.1), custom_call_target="tpu_custom_call" | custom-call | tf_op jit(solution)/shard_map/pallas_call | solution.py:254
  212.8 3.4 %copy.4 = bf16[8192,512]{1,0:T(8,128)(2,1)} copy(bf16[8192,512]{1,0:T(8,128)(2,1)S(1)} %shard_map.28) | data formatting | bytes 16777216
Async XLA Ops:
  0.0 0.7 copy-start

commit v5 on v4

--- a/solution.py
+++ b/solution.py
@@ -12,6 +12,7 @@
 CHUNK = 128
 TILE = 512
 EARLY = 256
+LATE = 128
 PIECES = ((0, 128), (128, 128))
 F32 = jnp.float32
 BF16 = jnp.bfloat16
@@ -65,8 +66,8 @@
     far_peer = {"samp": lax.rem(samp + 2, 4)}
     height, width = kept.shape
     low, high = pl.ds(0, width), pl.ds(width, width)
-    early = pl.ds(0, EARLY)
-    n_early, n_chunks = EARLY // CHUNK, height // CHUNK
+    early, late, aside = pl.ds(0, EARLY), pl.ds(EARLY, LATE), pl.ds(0, EARLY + LATE)
+    n_early, n_aside, n_chunks = EARLY // CHUNK, (EARLY + LATE) // CHUNK, height // CHUNK
 
     def rows_of(i, size=CHUNK):
         return pl.ds(pl.multiple_of(i * size, size), size)
@@ -84,9 +85,9 @@
         )
 
     n_loads = load_sem.shape[0]
-    part = height // n_loads
+    load_rows = height // n_loads
     loads = [
-        pltpu.make_async_copy(y_hbm.at[pl.ds(i * part, part)], y_ref.at[pl.ds(i * part, part)], load_sem.at[i])
+        pltpu.make_async_copy(y_hbm.at[pl.ds(i * load_rows, load_rows)], y_ref.at[pl.ds(i * load_rows, load_rows)], load_sem.at[i])
         for i in range(n_loads)
     ]
     for load in loads:
@@ -98,34 +99,41 @@
     for where in greeted:
         pl.semaphore_signal(barrier, inc=1, device_id=where, device_id_type=MESH)
 
+    core = lax.rem(samp, 2)
+    part = width // 2
+    my_part = pl.ds(pl.multiple_of(core * part, part), part)
+    peer_part = pl.ds(pl.multiple_of((1 - core) * part, part), part)
+
+    def exchange(source, target, step, kind, where):
+        n = kind + 5 * step
+        return remote(source, target, ex_send.at[n], ex_recv.at[n], where)
+
+    def passed_gram(step):
+        return exchange(gram_out.at[step, my_part], gram_in.at[step, my_part], step, 2, ahead)
+
     def summed_gram(step):
-        near = remote(acc, wide_in.at[step], ex_send.at[4 * step], ex_recv.at[4 * step], core_peer)
+        near = exchange(acc.at[peer_part], wide_in.at[step], step, 0, core_peer)
         near.start()
         near.wait()
-        chip = (acc[...] + wide_in[step]).astype(BF16)
+        chip = (acc[my_part, :] + wide_in[step]).astype(BF16)
         narrow_out[step] = chip
-        far = remote(
-            narrow_out.at[step], narrow_in.at[step], ex_send.at[4 * step + 1], ex_recv.at[4 * step + 1], far_peer
-        )
+        far = exchange(narrow_out.at[step], narrow_in.at[step], step, 1, far_peer)
         far.start()
         far.wait()
-        total = (chip.astype(F32) + narrow_in[step].astype(F32)).astype(BF16)
-        gram_out[step] = total
-        passed_gram(step).start()
+        gram_out[step, my_part] = (chip.astype(F32) + narrow_in[step].astype(F32)).astype(BF16)
+        share = exchange(gram_out.at[step, my_part], gram_out.at[step, my_part], step, 3, core_peer)
+        share.start()
         if step == 0:
             early_move(1).start()
-
-    core = lax.rem(samp, 2)
-    my_part = pl.ds(pl.multiple_of(core * (width // 2), width // 2), width // 2)
-
-    def passed_gram(step):
-        source, target = gram_out.at[step, my_part], gram_in.at[step, my_part]
-        return remote(source, target, ex_send.at[4 * step + 2], ex_recv.at[4 * step + 2], ahead)
+        else:
+            late_move.start()
+        passed_gram(step).start()
+        share.wait()
 
     def gram_from_behind(step):
         passed_gram(step).wait()
         half_gram = gram_in.at[step, my_part]
-        share = remote(half_gram, half_gram, ex_send.at[4 * step + 3], ex_recv.at[4 * step + 3], core_peer)
+        share = exchange(half_gram, half_gram, step, 4, core_peer)
         share.start()
         share.wait()
 
@@ -133,7 +141,8 @@
         rows = pl.ds(*PIECES[k])
         return remote(y_hbm.at[rows], early_in.at[rows], early_send.at[k], early_recv.at[k], ahead)
 
-    side_move = remote(moving.at[early], side_in, side_send, side_recv, side)
+    side_move = remote(moving.at[aside], side_in, side_send.at[0], side_recv.at[0], side)
+    late_move = remote(kept.at[late], early_kept.at[late], side_send.at[1], side_recv.at[1], ahead)
 
     def first_move(i):
         return remote(moving.at[rows_of(i)], arrived.at[rows_of(i)], send_sem.at[0, i], recv_sem.at[0, i], ahead)
@@ -154,7 +163,7 @@
         acc[...] = jnp.zeros_like(acc)
         for i in range(n_loads):
             loads[i].wait()
-            rows = pl.ds(i * part, part)
+            rows = pl.ds(i * load_rows, load_rows)
             acc[...] += over_rows(y_ref[rows, low], y_ref[rows, high])
             if i == 0:
                 tour_load.wait()
@@ -213,7 +222,7 @@
     @stage("moves1")
     def _():
 
-        @pl.loop(n_early, n_chunks)
+        @pl.loop(n_aside, n_chunks)
         def _(i):
             rotate_second(kept, arrived, move_cols, moved, low, rows_of(i))
             second_move(i).start()
@@ -231,7 +240,8 @@
     @stage("side")
     def _():
         side_move.wait()
-        rotate_second(early_kept, side_in, far_move, out_ref, high, early)
+        late_move.wait()
+        rotate_second(early_kept, side_in, far_move, out_ref, high, aside)
 
     @stage("last")
     def _():
@@ -239,6 +249,9 @@
         @pl.loop(n_early, n_chunks)
         def _(i):
             first_move(i).wait_send()
+
+        @pl.loop(n_aside, n_chunks)
+        def _(i):
             second_move(i).wait()
 
 
@@ -246,24 +259,25 @@
     height, columns = matrix.shape
     width = columns // 2
     block = pltpu.VMEM((height, width), BF16)
-    short = pltpu.VMEM((EARLY, width), BF16)
+    short = pltpu.VMEM((EARLY + LATE, width), BF16)
     cols = pltpu.VMEM((columns, width), BF16)
     grams = pltpu.VMEM((2, width, width), BF16)
+    halves = pltpu.VMEM((2, width // 2, width), BF16)
     copies = pltpu.SemaphoreType.DMA((2, height // CHUNK))
     one = pltpu.SemaphoreType.DMA
     return pl.pallas_call(
         kernel,
         out_shape=pltpu.VMEM((height, columns), BF16),
-        in_specs=[pl.BlockSpec(memory_space=pl.ANY), pl.BlockSpec(memory_space=pl.ANY)],
+        in_specs=[pl.BlockSpec(memory_space=pltpu.HBM), pl.BlockSpec(memory_space=pl.ANY)],
         out_specs=pl.BlockSpec(memory_space=pltpu.VMEM),
         scratch_shapes=[
             pltpu.SMEM(tournament.shape, jnp.int32), pltpu.SemaphoreType.DMA,
             pltpu.VMEM((height, columns), BF16), block, block, block, block,
             pltpu.VMEM((EARLY, columns), BF16), short, short, cols, cols, cols, cols,
-            pltpu.VMEM((width, width), F32), pltpu.VMEM((2, width, width), F32), grams, grams, grams, grams,
+            pltpu.VMEM((width, width), F32), pltpu.VMEM((2, width // 2, width), F32), halves, halves, grams, grams,
             pltpu.SemaphoreType.DMA((4,)), copies, copies,
-            pltpu.SemaphoreType.DMA((8,)), pltpu.SemaphoreType.DMA((8,)),
-            one((len(PIECES),)), one((len(PIECES),)), one, one,
+            pltpu.SemaphoreType.DMA((10,)), pltpu.SemaphoreType.DMA((10,)),
+            one((len(PIECES),)), one((len(PIECES),)), one((2,)), one((2,)),
         ],
         compiler_params=pltpu.CompilerParams(
             collective_id=0, has_side_effects=True, vmem_limit_bytes=40 * 1024 * 1024

time: 217 us -> 214 us (0.986)
  Pallas kernels: 212 us -> 209 us
    pallas_call x1, Pallas kernels: 212 us -> 209 us  [shards(): pl.pallas_call(kernel, out_shape=pltpu.VMEM((height, columns), BF16), in_...]
where the time goes in v5:
time: 214 us
  Pallas kernels  209 us (98%)
  local copies, waits for them, and re-layouts  4.08 us (2%)
    pallas_call x1, Pallas kernels, shards(): pl.pallas_call(kernel, out_shape=pltpu.VMEM((height, columns), BF16), in_...  209 us

profile of v5, /device:TPU:32, one launch (start us, length us, event | category | flops | bytes accessed | tf_op | source)
XLA Modules:
  0.0 213.5 jit_solution(11624342274453754568)
XLA Ops:
  0.0 0.0 copy-start
  0.0 0.7 copy-done
  0.7 209.4 %shard_map.28 = bf16[8192,512]{1,0:T(8,128)(2,1)S(1)} custom-call(s32[2,32]{1,0:T(2,128)S(1)} %copy-done, bf16[8192,512]{1,0:T(8,128)(2,1)} %y_hbm.1), custom_call_target="tpu_custom_call" | custom-call | tf_op jit(solution)/shard_map/pallas_call | solution.py:268
  210.1 3.4 %copy.4 = bf16[8192,512]{1,0:T(8,128)(2,1)} copy(bf16[8192,512]{1,0:T(8,128)(2,1)S(1)} %shard_map.28) | data formatting | bytes 16777216
Async XLA Ops:
  0.0 0.7 copy-start

commit v6 on v5

--- a/solution.py
+++ b/solution.py
@@ -12,7 +12,7 @@
 CHUNK = 128
 TILE = 512
 EARLY = 256
-LATE = 128
+LATE = 256
 PIECES = ((0, 128), (128, 128))
 F32 = jnp.float32
 BF16 = jnp.bfloat16
@@ -66,7 +66,7 @@
     far_peer = {"samp": lax.rem(samp + 2, 4)}
     height, width = kept.shape
     low, high = pl.ds(0, width), pl.ds(width, width)
-    early, late, aside = pl.ds(0, EARLY), pl.ds(EARLY, LATE), pl.ds(0, EARLY + LATE)
+    early, aside = pl.ds(0, EARLY), pl.ds(0, EARLY + LATE)
     n_early, n_aside, n_chunks = EARLY // CHUNK, (EARLY + LATE) // CHUNK, height // CHUNK
 
     def rows_of(i, size=CHUNK):
@@ -126,7 +126,7 @@
         if step == 0:
             early_move(1).start()
         else:
-            late_move.start()
+            late_move(1).start()
         passed_gram(step).start()
         share.wait()
 
@@ -142,7 +142,10 @@
         return remote(y_hbm.at[rows], early_in.at[rows], early_send.at[k], early_recv.at[k], ahead)
 
     side_move = remote(moving.at[aside], side_in, side_send.at[0], side_recv.at[0], side)
-    late_move = remote(kept.at[late], early_kept.at[late], side_send.at[1], side_recv.at[1], ahead)
+
+    def late_move(k):
+        rows = pl.ds(EARLY + k * (LATE // 2), LATE // 2)
+        return remote(kept.at[rows], early_kept.at[rows], side_send.at[1 + k], side_recv.at[1 + k], ahead)
 
     def first_move(i):
         return remote(moving.at[rows_of(i)], arrived.at[rows_of(i)], send_sem.at[0, i], recv_sem.at[0, i], ahead)
@@ -190,6 +193,8 @@
         def _(i):
             rotate_first(y_ref, keep_cols, kept, rows_of(i, TILE))
 
+        late_move(0).start()
+
     @stage("gwait0")
     def _():
         gram_from_behind(0)
@@ -240,7 +245,8 @@
     @stage("side")
     def _():
         side_move.wait()
-        late_move.wait()
+        late_move(0).wait()
+        late_move(1).wait()
         rotate_second(early_kept, side_in, far_move, out_ref, high, aside)
 
     @stage("last")
@@ -277,10 +283,10 @@
             pltpu.VMEM((width, width), F32), pltpu.VMEM((2, width // 2, width), F32), halves, halves, grams, grams,
             pltpu.SemaphoreType.DMA((4,)), copies, copies,
             pltpu.SemaphoreType.DMA((10,)), pltpu.SemaphoreType.DMA((10,)),
-            one((len(PIECES),)), one((len(PIECES),)), one((2,)), one((2,)),
+            one((len(PIECES),)), one((len(PIECES),)), one((3,)), one((3,)),
         ],
         compiler_params=pltpu.CompilerParams(
-            collective_id=0, has_side_effects=True, vmem_limit_bytes=40 * 1024 * 1024
+            collective_id=0, has_side_effects=True, vmem_limit_bytes=56_000_000
         ),
     )(tournament, matrix)
 

time: 214 us -> 212 us (level)
  no operation moved by 1% of the time
where the time goes in v6:
time: 212 us
  Pallas kernels  209 us (99%)
  local copies, waits for them, and re-layouts  3.4 us (2%)
    pallas_call x1, Pallas kernels, shards(): pl.pallas_call(kernel, out_shape=pltpu.VMEM((height, columns), BF16), in_...  209 us

profile of v6, /device:TPU:32, one launch (start us, length us, event | category | flops | bytes accessed | tf_op | source)
XLA Modules:
  0.0 212.0 jit_solution(9962874096341884468)
XLA Ops:
  0.0 208.6 %shard_map.28 = bf16[8192,512]{1,0:T(8,128)(2,1)S(1)} custom-call(s32[2,32]{1,0:T(2,128)} %tour_hbm.1, bf16[8192,512]{1,0:T(8,128)(2,1)} %y_hbm.1), custom_call_target="tpu_custom_call" | custom-call | tf_op jit(solution)/shard_map/pallas_call | solution.py:274
  208.6 3.4 %copy.4 = bf16[8192,512]{1,0:T(8,128)(2,1)} copy(bf16[8192,512]{1,0:T(8,128)(2,1)S(1)} %shard_map.28) | data formatting | bytes 16777216

commit v7 on v6

--- a/solution.py
+++ b/solution.py
@@ -9,7 +9,7 @@
 MESH = pl.DeviceIdType.MESH
 COUPLING = 2.0
 START_SCALE = 6.0
-CHUNK = 128
+CHUNK = 512
 TILE = 512
 EARLY = 256
 LATE = 256
@@ -67,7 +67,8 @@
     height, width = kept.shape
     low, high = pl.ds(0, width), pl.ds(width, width)
     early, aside = pl.ds(0, EARLY), pl.ds(0, EARLY + LATE)
-    n_early, n_aside, n_chunks = EARLY // CHUNK, (EARLY + LATE) // CHUNK, height // CHUNK
+    n_aside, n_chunks = (EARLY + LATE) // CHUNK, height // CHUNK
+    head = pl.ds(EARLY, LATE)
 
     def rows_of(i, size=CHUNK):
         return pl.ds(pl.multiple_of(i * size, size), size)
@@ -147,8 +148,11 @@
         rows = pl.ds(EARLY + k * (LATE // 2), LATE // 2)
         return remote(kept.at[rows], early_kept.at[rows], side_send.at[1 + k], side_recv.at[1 + k], ahead)
 
-    def first_move(i):
-        return remote(moving.at[rows_of(i)], arrived.at[rows_of(i)], send_sem.at[0, i], recv_sem.at[0, i], ahead)
+    def first_move(i, rows=None):
+        rows = rows_of(i) if rows is None else rows
+        return remote(moving.at[rows], arrived.at[rows], send_sem.at[0, i], recv_sem.at[0, i], ahead)
+
+    head_move = first_move(0, head)
 
     def second_move(i):
         return remote(
@@ -182,7 +186,10 @@
     @stage("moves0")
     def _():
 
-        @pl.loop(n_early, n_chunks)
+        rotate_first(y_ref, move_cols, moving, head)
+        head_move.start()
+
+        @pl.loop(n_aside, n_chunks)
         def _(i):
             rotate_first(y_ref, move_cols, moving, rows_of(i))
             first_move(i).start()
@@ -212,7 +219,10 @@
     @stage("gram1")
     def _():
 
-        @pl.loop(n_early, n_chunks)
+        head_move.wait_recv()
+        acc[...] += over_rows(kept[head, :], arrived[head, :])
+
+        @pl.loop(n_aside, n_chunks)
         def _(i):
             first_move(i).wait_recv()
             acc[...] += over_rows(kept[rows_of(i), :], arrived[rows_of(i), :])
@@ -252,12 +262,11 @@
     @stage("last")
     def _():
 
-        @pl.loop(n_early, n_chunks)
+        head_move.wait_send()
+
+        @pl.loop(n_aside, n_chunks)
         def _(i):
             first_move(i).wait_send()
-
-        @pl.loop(n_aside, n_chunks)
-        def _(i):
             second_move(i).wait()
 
 

time: 212 us -> 211 us (level)
  no operation moved by 1% of the time
where the time goes in v7:
time: 211 us; the launch traced here: 210 us
  Pallas kernels  207 us (98%)
  local copies, waits for them, and re-layouts  3.4 us (2%)
    pallas_call x1, Pallas kernels, shards(): pl.pallas_call(kernel, out_shape=pltpu.VMEM((height, columns), BF16), in_...  207 us

profile of v7, /device:TPU:32, one launch (start us, length us, event | category | flops | bytes accessed | tf_op | source)
XLA Modules:
  0.0 210.5 jit_solution(9358727704940046446)
XLA Ops:
  0.0 207.0 %shard_map.28 = bf16[8192,512]{1,0:T(8,128)(2,1)S(1)} custom-call(s32[2,32]{1,0:T(2,128)} %tour_hbm.1, bf16[8192,512]{1,0:T(8,128)(2,1)} %y_hbm.1), custom_call_target="tpu_custom_call" | custom-call | tf_op jit(solution)/shard_map/pallas_call | solution.py:283
  207.1 3.4 %copy.4 = bf16[8192,512]{1,0:T(8,128)(2,1)} copy(bf16[8192,512]{1,0:T(8,128)(2,1)S(1)} %shard_map.28) | data formatting | bytes 16777216

commit v8 on v7

--- a/solution.py
+++ b/solution.py
@@ -13,6 +13,7 @@
 TILE = 512
 EARLY = 256
 LATE = 256
+LATE_PIECES = ((0, 64), (64, 192))
 PIECES = ((0, 128), (128, 128))
 F32 = jnp.float32
 BF16 = jnp.bfloat16
@@ -145,7 +146,8 @@
     side_move = remote(moving.at[aside], side_in, side_send.at[0], side_recv.at[0], side)
 
     def late_move(k):
-        rows = pl.ds(EARLY + k * (LATE // 2), LATE // 2)
+        start, count = LATE_PIECES[k]
+        rows = pl.ds(EARLY + start, count)
         return remote(kept.at[rows], early_kept.at[rows], side_send.at[1 + k], side_recv.at[1 + k], ahead)
 
     def first_move(i, rows=None):

time: 211 us -> 211 us (level)
  no operation moved by 1% of the time
where the time goes in v8:
time: 211 us
  Pallas kernels  207 us (98%)
  local copies, waits for them, and re-layouts  3.4 us (2%)
    pallas_call x1, Pallas kernels, shards(): pl.pallas_call(kernel, out_shape=pltpu.VMEM((height, columns), BF16), in_...  207 us

profile of v8, /device:TPU:32, one launch (start us, length us, event | category | flops | bytes accessed | tf_op | source)
XLA Modules:
  0.0 210.7 jit_solution(8342488677116313916)
XLA Ops:
  0.0 207.3 %shard_map.28 = bf16[8192,512]{1,0:T(8,128)(2,1)S(1)} custom-call(s32[2,32]{1,0:T(2,128)} %tour_hbm.1, bf16[8192,512]{1,0:T(8,128)(2,1)} %y_hbm.1), custom_call_target="tpu_custom_call" | custom-call | tf_op jit(solution)/shard_map/pallas_call | solution.py:285
  207.3 3.4 %copy.4 = bf16[8192,512]{1,0:T(8,128)(2,1)} copy(bf16[8192,512]{1,0:T(8,128)(2,1)S(1)} %shard_map.28) | data formatting | bytes 16777216
